TPU v7x, 32 devices: a whole 2x2x4 slice. The times are simulated.
32 devices in a mesh: chan: 4 (over x, core), rad: 8 (over z, y).
Axes of the slice: x: 2, y: 2, z: 4, core: 2. Of those that a mesh axis runs over, the one named last changes fastest.
Arguments:
- psi: float32 [2, 768, 128, 128], P(None, 'chan', 'rad'), may hold values from -6 to 6
- k_prev: float32 [2, 768, 128, 128], P(None, 'chan', 'rad'), may hold values from -6 to 6
- gaunt: bfloat16 [4, 768, 768], replicated, may hold values from -0.875 to 0.875
- dipole: bfloat16 [768, 768], replicated, may hold values from -0.875 to 0.875
- kinetic: float32 [128, 128], replicated, as said below
- chan_l: int32 [768, 2], P('chan'), may hold values from 0 to 23
- field_amp: float32 [1], replicated, may hold values from 0.02 to 0.1
Outputs:
- deriv: float32 [2, 768, 128, 128], P(None, 'chan', 'rad')
Inputs may be any that keep to these rules, and one draw needn't show every extreme that they name: `kinetic`: symmetric; zero where the row's and the column's blocks of 16 indices are more than one block apart.
All inputs are finite; a program needn't handle non-finite values.
Results may differ from a plain program's by a relative error of at most 0.00037.
Values may be sent and summed in bfloat16 or wider, within the bound.
A program may use at most 64 MiB of HBM per device.

v0:
```python
import jax
import jax.numpy as jnp
from jax import lax
from jax.sharding import PartitionSpec as P


def extended(array, sides, width):
    for axis, dim in sides:
        peers, length = (lax.axis_size(axis), array.shape[dim])
        up = [(i, (i + 1) % peers) for i in range(peers - 1)]
        down = [(j, i) for i, j in up]
        last = lax.slice_in_dim(array, length - width, length, axis=dim)
        initial = lax.slice_in_dim(array, 0, width, axis=dim)
        before = lax.ppermute(last, axis, up)
        after = lax.ppermute(initial, axis, down)
        array = jnp.concatenate([before, array, after], axis=dim)
    return array


def on_device(psi, k_prev, gaunt, dipole, kinetic, chan_l, field_amp):
    highest = lax.Precision.HIGHEST
    section = psi + 0.5 * k_prev
    local_chan = section.shape[1]
    rows = section.shape[2]
    width = section.shape[3]
    rad_at = lax.axis_index("rad")
    first_r = (
        1.0 + 8.0 * (rad_at * rows + jnp.arange(rows, dtype=jnp.int32)).astype(jnp.float32) / width
    )
    second_r = 1.0 + 8.0 * jnp.arange(width, dtype=jnp.float32) / width
    along_r2 = jnp.einsum("acij,kj->acik", section, kinetic, precision=highest)
    padded = extended(section.astype(jnp.bfloat16), (("rad", 2),), rows).astype(section.dtype)
    band = lax.dynamic_slice_in_dim(kinetic, rad_at * rows, rows, 0)
    widened = jnp.pad(band, ((0, 0), (rows, rows)))
    local_band = lax.dynamic_slice_in_dim(widened, rad_at * rows, 3 * rows, 1)
    along_r1 = jnp.einsum("ij,acjk->acik", local_band, padded, precision=highest)
    lvals = chan_l.astype(jnp.float32)
    first_l = lvals[:, 0] * (lvals[:, 0] + 1.0)
    second_l = lvals[:, 1] * (lvals[:, 1] + 1.0)
    potential = (
        first_l[:, None, None] / (2.0 * first_r * first_r)[None, :, None]
        + second_l[:, None, None] / (2.0 * second_r * second_r)[None, None, :]
        - 2.0 / first_r[None, :, None]
        - 2.0 / second_r[None, None, :]
    )
    sent = section.astype(jnp.bfloat16).reshape(2, local_chan, rows * width)
    chan_at = lax.axis_index("chan")
    block = lax.all_to_all(sent, "chan", split_axis=2, concat_axis=1, tiled=True)
    count = block.shape[2]
    place = chan_at * count + jnp.arange(count, dtype=jnp.int32)
    row_r = 1.0 + 8.0 * (rad_at * rows + place // width).astype(jnp.float32) / width
    col_r = 1.0 + 8.0 * (place % width).astype(jnp.float32) / width
    far = jnp.maximum(row_r, col_r)
    near = jnp.minimum(row_r, col_r)
    inverse = 1.0 / far
    ratio = near * inverse
    power = inverse
    total = jnp.zeros(block.shape, jnp.float32)
    for order in range(gaunt.shape[0]):
        mixed = jnp.einsum("cd,adq->acq", gaunt[order], block, preferred_element_type=jnp.float32)
        total = total + power[None, None, :] * mixed
        power = power * ratio
    mixed = jnp.einsum("cd,adq->acq", dipole, block, preferred_element_type=jnp.float32)
    total = total + (field_amp[0] * (row_r + col_r))[None, None, :] * mixed
    coupled = lax.all_to_all(
        total.astype(jnp.bfloat16), "chan", split_axis=1, concat_axis=2, tiled=True
    )
    coupled = coupled.reshape(coupled.shape[0], local_chan, rows, width)
    ham = along_r1 + along_r2 + potential[None] * section + coupled.astype(jnp.float32)
    return jnp.stack([ham[1], -ham[0]])


def solution(mesh):
    placed = (
        P(None, "chan", "rad", None),
        P(None, "chan", "rad", None),
        P(),
        P(),
        P(),
        P("chan", None),
        P(),
    )
    return jax.shard_map(
        on_device,
        mesh=mesh,
        in_specs=placed,
        out_specs=P(None, "chan", "rad", None),
        check_vma=False,
    )
```

profile of v0, /device:TPU:0, one launch (start us, length us, event | category | flops | bytes accessed | tf_op | source)
XLA Modules:
  0.0 111.4 jit_solution(17644316627872621807)
XLA Ops:
  0.0 0.0 copy-start
  0.0 4.5 %fusion.45 = bf16[2,192,16,128]{3,2,1,0:T(8,128)(2,1)} fusion(f32[2,192,16,128]{3,2,1,0:T(8,128)} %param.7, f32[2,192,16,128]{3,2,1,0:T(8,128)} %param.8), kind=kLoop, calls=%fused_computation.70 | loop fusion | flops 2359296 | bytes 7864320 | tf_op jit(solution)/shard_map/convert_element_type | solution.py:32
  4.5 0.0 copy-start.2
  4.5 0.0 copy-start.1
  4.5 6.2 %collective-permute-start = (bf16[2,192,16,128]{3,2,1,0:T(8,128)(2,1)}, bf16[2,192,16,128]{3,2,1,0:T(8,128)(2,1)}, u32[]{:S(2)}, u32[]{:S(2)}) collective-permute-start(bf16[2,192,16,128]{3,2,1,0:T(8,128)(2,1)} %fusion.45), channel_id=1, source_target_pairs={{0,1},{1,2},{2,3},{3,4},{4,5},{5,6},{6,7},{8,9},{9,10},{10,11},{11... | collective-permute-start | bytes 4718600 | tf_op jit(solution)/shard_map/ppermute | solution.py:14
  10.7 1.3 %collective-permute-start.1 = (bf16[2,192,16,128]{3,2,1,0:T(8,128)(2,1)}, bf16[2,192,16,128]{3,2,1,0:T(8,128)(2,1)}, u32[]{:S(2)}, u32[]{:S(2)}) collective-permute-start(bf16[2,192,16,128]{3,2,1,0:T(8,128)(2,1)} %fusion.45), channel_id=1, source_target_pairs={{1,0},{2,1},{3,2},{4,3},{5,4},{6,5},{7,6},{9,8},{10,9},{11,10},{12... | collective-permute-start | bytes 4718600 | tf_op jit(solution)/shard_map/ppermute | solution.py:15
  12.0 4.6 %copy.43 = bf16[2,192,16,128]{1,0,3,2:T(2,128)(2,1)} copy(bf16[2,192,16,128]{3,2,1,0:T(8,128)(2,1)} %fusion.45) | data formatting | bytes 3145728 | tf_op jit(solution)/shard_map/reshape | solution.py:46
  16.6 3.6 %all-to-all-start = ((bf16[2,192,2048]{1,0,2:T(2,128)(2,1)}), bf16[2,192,2048]{1,0,2:T(2,128)(2,1)S(1)}, u32[]{:S(2)}, u32[]{:S(2)}) async-start(bf16[2,192,2048]{1,0,2:T(2,128)(2,1)} %bitcast.55), calls=%async_computation | async-start | bytes 4194304 | tf_op jit(solution)/shard_map/all_to_all | solution.py:48
  20.9 0.0 copy-done.2
  21.0 0.0 copy-done.1
  21.1 0.1 broadcast_divide_fusion.1
  21.2 24.7 %all-to-all-done = bf16[2,192,2048]{1,0,2:T(2,128)(2,1)S(1)} async-done(((bf16[2,192,2048]{1,0,2:T(2,128)(2,1)}), bf16[2,192,2048]{1,0,2:T(2,128)(2,1)S(1)}, u32[]{:S(2)}, u32[]{:S(2)}) %all-to-all-start) | async-done | bytes 1572896 | tf_op jit(solution)/shard_map/all_to_all | solution.py:48
  45.8 4.6 %copy.44 = bf16[2,192,4,512]{3,2,1,0:T(4,128)(2,1)} copy(bf16[2,192,4,512]{1,0,3,2:T(2,128)(2,1)S(1)} %bitcast.54) | data formatting | bytes 3145728 | tf_op jit(solution)/shard_map/all_to_all | solution.py:48
  50.5 0.0 slice-start
  50.5 1.9 %copy.27 = bf16[2,4,192,512]{3,2,1,0:T(8,128)(2,1)S(1)} copy(bf16[2,4,192,512]{3,1,2,0:T(4,128)(2,1)} %bitcast.56) | data formatting | bytes 3145728 | tf_op jit(solution)/shard_map/all_to_all | solution.py:48
  52.4 0.0 slice-start.1
  52.4 2.8 %fusion.12 = f32[2,512,768]{2,1,0:T(8,128)S(1)} fusion(bf16[2,768,512]{2,1,0:T(8,128)(2,1)S(1)} %bitcast.58, bf16[4,768,768]{2,1,0:T(8,128)(2,1)} %param.9), kind=kOutput, calls=%fused_computation.17 | convolution fusion | flops 1207959552 | bytes 5898240 | tf_op jit(solution)/shard_map/cd,adq->acq/dot_general | solution.py:60
  55.1 2.7 %fusion.14 = f32[2,512,768]{2,1,0:T(8,128)S(1)} fusion(bf16[2,768,512]{2,1,0:T(8,128)(2,1)S(1)} %bitcast.59, bf16[4,768,768]{2,1,0:T(8,128)(2,1)} %param.9), kind=kOutput, calls=%fused_computation.19 | convolution fusion | flops 1207959552 | bytes 5898240 | tf_op jit(solution)/shard_map/cd,adq->acq/dot_general | solution.py:60
  57.8 0.0 slice-done
  57.9 0.0 slice-done.1
  57.9 1.4 %fusion.16 = f32[2,512,768]{2,1,0:T(8,128)S(1)} fusion(bf16[2,768,512]{2,1,0:T(8,128)(2,1)S(1)} %bitcast.60, bf16[4,768,768]{2,1,0:T(8,128)(2,1)S(1)} %bitcast.66), kind=kOutput, calls=%fused_computation.21 | convolution fusion | flops 1207959552 | bytes 5898240 | tf_op jit(solution)/shard_map/cd,adq->acq/dot_general | solution.py:60
  59.3 1.4 %fusion.18 = f32[2,512,768]{2,1,0:T(8,128)S(1)} fusion(bf16[2,768,512]{2,1,0:T(8,128)(2,1)S(1)} %bitcast.61, bf16[4,768,768]{2,1,0:T(8,128)(2,1)S(1)} %bitcast.66), kind=kOutput, calls=%fused_computation.23 | convolution fusion | flops 1207959552 | bytes 5898240 | tf_op jit(solution)/shard_map/cd,adq->acq/dot_general | solution.py:60
  60.8 0.0 copy-done
  60.8 2.7 %fusion.10 = bf16[2,768,512]{1,2,0:T(8,128)(2,1)S(1)} fusion(bf16[2,768,512]{2,1,0:T(8,128)(2,1)S(1)} %bitcast.62, f32[512]{0:T(512)S(1)} %get-tuple-element.9, f32[2,512,768]{2,1,0:T(8,128)S(1)} %fusion.12, f32[512]{0:T(512)S(1)} %get-tuple-element.12, f32[2,512,768]{2,1,0:T(8,128)S(1)} %fusion.14, f32[512]{0:T(512)S(1)} %fusion.40, ...), kind=kOutput, calls=%fused_computation.15 | convolution fusion | flops 1215823872 | bytes 16918528 | tf_op jit(solution)/shard_map/cd,adq->acq/dot_general | solution.py:63
  63.4 3.0 %copy.33 = bf16[2,768,512]{2,0,1:T(2,128)(2,1)} copy(bf16[2,768,512]{1,2,0:T(8,128)(2,1)S(1)} %fusion.10) | data formatting | bytes 3145728 | tf_op jit(solution)/shard_map/convert_element_type | solution.py:66
  66.5 4.5 %all-to-all-start.1 = ((bf16[2,768,512]{2,0,1:T(2,128)(2,1)}), bf16[2,768,512]{2,0,1:T(2,128)(2,1)}, u32[]{:S(2)}, u32[]{:S(2)}) async-start(bf16[2,768,512]{2,0,1:T(2,128)(2,1)} %copy.33), calls=%async_computation.1 | async-start | bytes 3145728 | tf_op jit(solution)/shard_map/all_to_all | solution.py:65
  71.0 0.1 broadcast_divide_fusion
  71.1 0.5 subtract_subtract_fusion
  71.6 5.9 %fusion.24 = f32[2,192,16,128]{3,2,1,0:T(8,128)} fusion(f32[128,128]{1,0:T(8,128)S(1)} %copy-done.1, f32[2,192,16,128]{3,2,1,0:T(8,128)} %param.7, f32[2,192,16,128]{3,2,1,0:T(8,128)} %param.8), kind=kOutput, calls=%fused_computation.29 | convolution fusion | flops 1209532416 | bytes 9502720 | tf_op jit(solution)/shard_map/acij,kj->acik/dot_general | solution.py:31
  77.5 13.5 %all-to-all-done.1 = bf16[2,768,512]{2,0,1:T(2,128)(2,1)} async-done(((bf16[2,768,512]{2,0,1:T(2,128)(2,1)}), bf16[2,768,512]{2,0,1:T(2,128)(2,1)}, u32[]{:S(2)}, u32[]{:S(2)}) %all-to-all-start.1) | async-done | bytes 1572896 | tf_op jit(solution)/shard_map/all_to_all | solution.py:65
  90.9 1.7 %copy.34 = bf16[2,768,512]{2,1,0:T(8,128)(2,1)S(1)} copy(bf16[2,768,512]{2,0,1:T(2,128)(2,1)} %all-to-all-done.1) | data formatting | bytes 3145728 | tf_op jit(solution)/shard_map/all_to_all | solution.py:65
  92.6 0.4 convert_bitcast_fusion
  93.0 3.7 %copy.35 = f32[2,192,4,512]{3,2,1,0:T(4,128)} copy(f32[2,192,4,512]{3,1,2,0:T(8,128)S(1)} %convert_bitcast_fusion) | data formatting | bytes 6291456 | tf_op jit(solution)/shard_map/convert_element_type | solution.py:69
  96.7 5.1 %reshape.171 = f32[2,192,16,128]{3,2,1,0:T(8,128)} reshape(f32[2,192,4,512]{3,2,1,0:T(4,128)} %copy.35) | data formatting | bytes 6291456 | tf_op jit(solution)/shard_map/convert_element_type | solution.py:69
  101.8 0.0 copy-start.3
  101.8 0.0 collective-permute-done
  101.8 0.0 collective-permute-done.1
  101.8 7.6 %fusion.7 = f32[2,192,16,128]{3,2,1,0:T(8,128)S(1)} fusion(f32[2,192,16,128]{3,2,1,0:T(8,128)} %reshape.171, f32[2,192,16,128]{3,2,1,0:T(8,128)} %fusion.24, bf16[2,192,16,128]{3,2,1,0:T(8,128)(2,1)} %collective-permute-done.1, bf16[2,192,16,128]{3,2,1,0:T(8,128)(2,1)} %fusion.45, bf16[2,192,16,128]{3,2,1,0:T(8,128)(2,1)} %collective-permute-done, ...), kind=kOutput, calls=%fused_computation.10 | convolution fusion | flops 471859200 | bytes 22028292 | tf_op jit(solution)/shard_map/ij,acjk->acik/dot_general | solution.py:36
  109.4 0.0 copy-done.3
  109.4 0.3 fusion.46
  109.7 0.0 copy-start.4
  109.7 1.7 %copy-done.4 = f32[2,192,16,128]{3,2,1,0:T(8,128)} copy-done((f32[2,192,16,128]{3,2,1,0:T(8,128)}, f32[2,192,16,128]{3,2,1,0:T(8,128)S(1)}, u32[]{:S(2)}) %copy-start.4) | copy-done | bytes 3145752
  (14 shorter events, 0.1 us)
Async XLA Ops:
  0.0 60.8 %copy-start = (bf16[768,768]{1,0:T(8,128)(2,1)S(1)}, bf16[768,768]{1,0:T(8,128)(2,1)}, u32[]{:S(2)}) copy-start(bf16[768,768]{1,0:T(8,128)(2,1)} %param.10) | copy-start | bytes 3538948
  4.5 16.4 %copy-start.2 = (s32[192,2]{0,1:T(2,128)S(1)}, s32[192,2]{0,1:T(2,128)}, u32[]{:S(2)}) copy-start(s32[192,2]{0,1:T(2,128)} %param.12) | copy-start | bytes 4612
  4.5 16.5 %copy-start.1 = (f32[128,128]{1,0:T(8,128)S(1)}, f32[128,128]{1,0:T(8,128)}, u32[]{:S(2)}) copy-start(f32[128,128]{1,0:T(8,128)} %param.11) | copy-start | bytes 196612
  4.5 97.3 %collective-permute-start = (bf16[2,192,16,128]{3,2,1,0:T(8,128)(2,1)}, bf16[2,192,16,128]{3,2,1,0:T(8,128)(2,1)}, u32[]{:S(2)}, u32[]{:S(2)}) collective-permute-start(bf16[2,192,16,128]{3,2,1,0:T(8,128)(2,1)} %fusion.45), channel_id=1, source_target_pairs={{0,1},{1,2},{2,3},{3,4},{4,5},{5,6},{6,7},{8,9},{9,10},{10,11},{11... | collective-permute-start | bytes 4718600 | tf_op jit(solution)/shard_map/ppermute | solution.py:14
  10.7 91.1 %collective-permute-start.1 = (bf16[2,192,16,128]{3,2,1,0:T(8,128)(2,1)}, bf16[2,192,16,128]{3,2,1,0:T(8,128)(2,1)}, u32[]{:S(2)}, u32[]{:S(2)}) collective-permute-start(bf16[2,192,16,128]{3,2,1,0:T(8,128)(2,1)} %fusion.45), channel_id=1, source_target_pairs={{1,0},{2,1},{3,2},{4,3},{5,4},{6,5},{7,6},{9,8},{10,9},{11,10},{12... | collective-permute-start | bytes 4718600 | tf_op jit(solution)/shard_map/ppermute | solution.py:15
  16.6 29.2 %all-to-all-start = ((bf16[2,192,2048]{1,0,2:T(2,128)(2,1)}), bf16[2,192,2048]{1,0,2:T(2,128)(2,1)S(1)}, u32[]{:S(2)}, u32[]{:S(2)}) async-start(bf16[2,192,2048]{1,0,2:T(2,128)(2,1)} %bitcast.55), calls=%async_computation | async-start | bytes 4194304 | tf_op jit(solution)/shard_map/all_to_all | solution.py:48
  50.5 7.4 %slice-start = ((s8[4718592]{0:T(1024)(128)(4,1)}), s8[4194304]{0:T(1024)(128)(4,1)S(1)}, s32[]{:S(2)}) async-start(s8[4718592]{0:T(1024)(128)(4,1)} %bitcast.65), calls=%async_computation.2 | async-start | bytes 8388608
  52.4 5.5 %slice-start.1 = ((s8[4718592]{0:T(1024)(128)(4,1)}), s8[524288]{0:T(1024)(128)(4,1)S(1)}, s32[]{:S(2)}) async-start(s8[4718592]{0:T(1024)(128)(4,1)} %bitcast.65), calls=%async_computation.3 | async-start | bytes 1048576
  66.5 24.5 %all-to-all-start.1 = ((bf16[2,768,512]{2,0,1:T(2,128)(2,1)}), bf16[2,768,512]{2,0,1:T(2,128)(2,1)}, u32[]{:S(2)}, u32[]{:S(2)}) async-start(bf16[2,768,512]{2,0,1:T(2,128)(2,1)} %copy.33), calls=%async_computation.1 | async-start | bytes 3145728 | tf_op jit(solution)/shard_map/all_to_all | solution.py:65
  101.8 7.6 %copy-start.3 = (f32[2,192,16,128]{3,2,1,0:T(8,128)S(1)}, f32[2,192,16,128]{3,2,1,0:T(8,128)}, u32[]{:S(2)}) copy-start(f32[2,192,16,128]{3,2,1,0:T(8,128)} %custom-call) | copy-start | bytes 9437188
  109.7 1.7 %copy-start.4 = (f32[2,192,16,128]{3,2,1,0:T(8,128)}, f32[2,192,16,128]{3,2,1,0:T(8,128)S(1)}, u32[]{:S(2)}) copy-start(f32[2,192,16,128]{3,2,1,0:T(8,128)S(1)} %get-tuple-element.17) | copy-start | bytes 9437188
where the time goes:
time: 112 us; the launch traced here: 111 us
  waiting for transfers between devices  38.1 us (34%)
  local copies, waits for them, and re-layouts  26.3 us (23%)
  matrix products  24.4 us (22%)
  starting transfers between devices  15.6 us (14%)
  other arithmetic  5.95 us (5%)
    all_to_all x1, waiting for transfers between devices, on_device(): lax.all_to_all(sent, 'chan', split_axis=2, concat_axis=1, tiled=True)  24.7 us
    all_to_all x1, waiting for transfers between devices, on_device(): lax.all_to_all(total.astype(jnp.bfloat16), 'chan', split_axis=1, concat_a...  13.5 us
    convert_element_type x2, local copies, waits for them, and re-layouts, on_device(): coupled.astype(jnp.float32)  8.79 us
    dot_general x4, matrix products, on_device(): jnp.einsum('cd,adq->acq', gaunt[order], block, preferred_element_type=jnp...  8.34 us
    dot_general x1, matrix products, on_device(): jnp.einsum('ij,acjk->acik', local_band, padded, precision=highest)  7.55 us
    all_to_all x2, local copies, waits for them, and re-layouts, on_device(): lax.all_to_all(sent, 'chan', split_axis=2, concat_axis=1, tiled=True)  6.5 us
    ppermute x1, starting transfers between devices, extended(): before = lax.ppermute(last, axis, up)  6.2 us
    dot_general x1, matrix products, on_device(): along_r2 = jnp.einsum('acij,kj->acik', section, kinetic, precision=highest)  5.87 us
  transfers between devices with their start and end apart: 4, of which 2 were waited for; matrix products, arithmetic and copies ran while one was open for 38% of the time, Pallas kernels for 0%

commit v1 on v0

--- a/solution.py
+++ b/solution.py
@@ -2,6 +2,12 @@
 import jax.numpy as jnp
 from jax import lax
 from jax.sharding import PartitionSpec as P
+
+
+def exchange_blocks(array, mesh_axis, split, join):
+    cells = jnp.split(array, lax.axis_size(mesh_axis), axis=split)
+    received = lax.all_to_all(jnp.stack(cells), mesh_axis, 0, 0)
+    return jnp.concatenate(received, axis=join)
 
 
 def extended(array, sides, width):
@@ -45,7 +51,7 @@
     )
     sent = section.astype(jnp.bfloat16).reshape(2, local_chan, rows * width)
     chan_at = lax.axis_index("chan")
-    block = lax.all_to_all(sent, "chan", split_axis=2, concat_axis=1, tiled=True)
+    block = exchange_blocks(sent, "chan", 2, 1)
     count = block.shape[2]
     place = chan_at * count + jnp.arange(count, dtype=jnp.int32)
     row_r = 1.0 + 8.0 * (rad_at * rows + place // width).astype(jnp.float32) / width

time: 112 us -> 99.3 us (0.89)
  local copies, waits for them, and re-layouts: 26.3 us -> 18 us
  waiting for transfers between devices: 38.1 us -> 32.5 us
  other arithmetic: 5.95 us -> 7.28 us
    all_to_all x2 -> x1, local copies, waits for them, and re-layouts: 6.5 us -> 0.16 us  [exchange_blocks(): received = lax.all_to_all(jnp.stack(cells), mesh_axis, 0, 0)]
    all_to_all x1, waiting for transfers between devices: 24.7 us -> 19 us  [exchange_blocks(): received = lax.all_to_all(jnp.stack(cells), mesh_axis, 0, 0)]
    reshape x1, local copies, waits for them, and re-layouts: 4.61 us -> 2.55 us  [on_device(): sent = section.astype(jnp.bfloat16).reshape(2, local_chan, rows * width)]
    another operation x0 -> x1, other arithmetic: none -> 1.34 us  [exchange_blocks(): received = lax.all_to_all(jnp.stack(cells), mesh_axis, 0, 0)]
  transfers between devices with their start and end apart: 4 -> 4, of which waited for: 2 -> 2; matrix products, arithmetic and copies ran while one was open for 38% -> 36% of each run, Pallas kernels for 0% -> 0%
where the time goes in v1:
time: 99.3 us; the launch traced here: 98.8 us
  waiting for transfers between devices  32.5 us (33%)
  matrix products  24.5 us (25%)
  local copies, waits for them, and re-layouts  18 us (18%)
  starting transfers between devices  15.5 us (16%)
  other arithmetic  7.28 us (7%)
    all_to_all x1, waiting for transfers between devices, exchange_blocks(): received = lax.all_to_all(jnp.stack(cells), mesh_axis, 0, 0)  19 us
    all_to_all x1, waiting for transfers between devices, on_device(): lax.all_to_all(total.astype(jnp.bfloat16), 'chan', split_axis=1, concat_a...  13.5 us
    convert_element_type x2, local copies, waits for them, and re-layouts, on_device(): coupled.astype(jnp.float32)  8.8 us
    dot_general x4, matrix products, on_device(): jnp.einsum('cd,adq->acq', gaunt[order], block, preferred_element_type=jnp...  8.43 us
    dot_general x1, matrix products, on_device(): jnp.einsum('ij,acjk->acik', local_band, padded, precision=highest)  7.55 us
    ppermute x1, starting transfers between devices, extended(): before = lax.ppermute(last, axis, up)  6.09 us
    dot_general x1, matrix products, on_device(): along_r2 = jnp.einsum('acij,kj->acik', section, kinetic, precision=highest)  5.88 us
    all_to_all x1, starting transfers between devices, on_device(): lax.all_to_all(total.astype(jnp.bfloat16), 'chan', split_axis=1, concat_a...  4.54 us
  transfers between devices with their start and end apart: 4, of which 2 were waited for; matrix products, arithmetic and copies ran while one was open for 36% of the time, Pallas kernels for 0%

profile of v1, /device:TPU:0, one launch (start us, length us, event | category | flops | bytes accessed | tf_op | source)
XLA Modules:
  0.0 98.8 jit_solution(3435289977082535660)
XLA Ops:
  0.0 0.0 copy-start
  0.0 4.5 %fusion.45 = bf16[2,192,16,128]{3,2,1,0:T(8,128)(2,1)} fusion(f32[2,192,16,128]{3,2,1,0:T(8,128)} %param.7, f32[2,192,16,128]{3,2,1,0:T(8,128)} %param.8), kind=kLoop, calls=%fused_computation.75 | loop fusion | flops 2359296 | bytes 7864320 | tf_op jit(solution)/shard_map/convert_element_type | solution.py:38
  4.5 6.1 %collective-permute-start = (bf16[2,192,16,128]{3,2,1,0:T(8,128)(2,1)}, bf16[2,192,16,128]{3,2,1,0:T(8,128)(2,1)}, u32[]{:S(2)}, u32[]{:S(2)}) collective-permute-start(bf16[2,192,16,128]{3,2,1,0:T(8,128)(2,1)} %fusion.45), channel_id=1, source_target_pairs={{0,1},{1,2},{2,3},{3,4},{4,5},{5,6},{6,7},{8,9},{9,10},{10,11},{11... | collective-permute-start | bytes 4718600 | tf_op jit(solution)/shard_map/ppermute | solution.py:20
  10.6 1.3 %collective-permute-start.1 = (bf16[2,192,16,128]{3,2,1,0:T(8,128)(2,1)}, bf16[2,192,16,128]{3,2,1,0:T(8,128)(2,1)}, u32[]{:S(2)}, u32[]{:S(2)}) collective-permute-start(bf16[2,192,16,128]{3,2,1,0:T(8,128)(2,1)} %fusion.45), channel_id=1, source_target_pairs={{1,0},{2,1},{3,2},{4,3},{5,4},{6,5},{7,6},{9,8},{10,9},{11,10},{12... | collective-permute-start | bytes 4718600 | tf_op jit(solution)/shard_map/ppermute | solution.py:21
  11.9 2.5 %reshape.176 = bf16[2,192,2048]{2,1,0:T(8,128)(2,1)S(1)} reshape(bf16[2,192,16,128]{3,2,1,0:T(8,128)(2,1)} %fusion.45) | data formatting | bytes 3145728 | tf_op jit(solution)/shard_map/reshape | solution.py:52
  14.4 0.1 slice_bitcast_fusion.3
  14.6 0.0 copy-start.2
  14.6 0.0 copy-start.1
  14.6 1.3 %pad_maximum_fusion.1 = bf16[4,2,192,512]{3,2,1,0:T(8,128)(2,1)} fusion(bf16[1,2,192,512]{3,2,1,0:T(8,128)(2,1)S(1)} %get-tuple-element.8, bf16[1,2,192,512]{3,2,1,0:T(8,128)(2,1)S(1)} %get-tuple-element.9, bf16[1,2,192,512]{3,2,1,0:T(8,128)(2,1)S(1)} %get-tuple-element.10, bf16[1,2,192,512]{3,2,1,0:T(8,128)(2,1)S(1)} %get-tuple-element.7), kind=kLoop, calls=%fused_computation.14 | loop fusion | flops 2359296 | bytes 3145728 | tf_op jit(solution)/shard_map/stack | solution.py:9
  15.9 3.6 %all-to-all-start = ((bf16[4,2,192,512]{3,2,1,0:T(8,128)(2,1)}), bf16[4,2,192,512]{3,2,1,0:T(8,128)(2,1)S(1)}, u32[]{:S(2)}, u32[]{:S(2)}) async-start(bf16[4,2,192,512]{3,2,1,0:T(8,128)(2,1)} %pad_maximum_fusion.1), calls=%async_computation | async-start | bytes 3145728 | tf_op jit(solution)/shard_map/all_to_all | solution.py:9
  20.2 0.0 copy-done.2
  20.3 0.0 copy-done.1
  20.4 0.1 broadcast_divide_fusion.1
  20.5 19.0 %all-to-all-done = bf16[4,2,192,512]{3,2,1,0:T(8,128)(2,1)S(1)} async-done(((bf16[4,2,192,512]{3,2,1,0:T(8,128)(2,1)}), bf16[4,2,192,512]{3,2,1,0:T(8,128)(2,1)S(1)}, u32[]{:S(2)}, u32[]{:S(2)}) %all-to-all-start) | async-done | bytes 1572896 | tf_op jit(solution)/shard_map/all_to_all | solution.py:9
  39.5 0.0 slice-start
  39.5 0.2 copy.20
  39.7 0.0 slice-start.1
  39.7 2.9 %fusion.12 = f32[2,512,768]{2,1,0:T(8,128)S(1)} fusion(bf16[2,768,512]{2,1,0:T(8,128)(2,1)S(1)} %bitcast.64, bf16[4,768,768]{2,1,0:T(8,128)(2,1)} %param.9), kind=kOutput, calls=%fused_computation.18 | convolution fusion | flops 1207959552 | bytes 5898240 | tf_op jit(solution)/shard_map/cd,adq->acq/dot_general | solution.py:66
  42.5 2.7 %fusion.14 = f32[2,512,768]{2,1,0:T(8,128)S(1)} fusion(bf16[2,768,512]{2,1,0:T(8,128)(2,1)S(1)} %bitcast.65, bf16[4,768,768]{2,1,0:T(8,128)(2,1)} %param.9), kind=kOutput, calls=%fused_computation.20 | convolution fusion | flops 1207959552 | bytes 5898240 | tf_op jit(solution)/shard_map/cd,adq->acq/dot_general | solution.py:66
  45.3 0.0 slice-done
  45.3 0.0 slice-done.1
  45.3 1.4 %fusion.16 = f32[2,512,768]{2,1,0:T(8,128)S(1)} fusion(bf16[2,768,512]{2,1,0:T(8,128)(2,1)S(1)} %bitcast.66, bf16[4,768,768]{2,1,0:T(8,128)(2,1)S(1)} %bitcast.72), kind=kOutput, calls=%fused_computation.22 | convolution fusion | flops 1207959552 | bytes 5898240 | tf_op jit(solution)/shard_map/cd,adq->acq/dot_general | solution.py:66
  46.7 1.4 %fusion.18 = f32[2,512,768]{2,1,0:T(8,128)S(1)} fusion(bf16[2,768,512]{2,1,0:T(8,128)(2,1)S(1)} %bitcast.67, bf16[4,768,768]{2,1,0:T(8,128)(2,1)S(1)} %bitcast.72), kind=kOutput, calls=%fused_computation.24 | convolution fusion | flops 1207959552 | bytes 5898240 | tf_op jit(solution)/shard_map/cd,adq->acq/dot_general | solution.py:66
  48.2 0.0 copy-done
  48.2 2.7 %fusion.10 = bf16[2,768,512]{1,2,0:T(8,128)(2,1)S(1)} fusion(bf16[2,768,512]{2,1,0:T(8,128)(2,1)S(1)} %bitcast.68, f32[512]{0:T(512)S(1)} %get-tuple-element.13, f32[2,512,768]{2,1,0:T(8,128)S(1)} %fusion.12, f32[512]{0:T(512)S(1)} %get-tuple-element.16, f32[2,512,768]{2,1,0:T(8,128)S(1)} %fusion.14, f32[512]{0:T(512)S(1)} %fusion.40, ...), kind=kOutput, calls=%fused_computation.16 | convolution fusion | flops 1215823872 | bytes 16918528 | tf_op jit(solution)/shard_map/cd,adq->acq/dot_general | solution.py:69
  50.8 3.0 %copy.26 = bf16[2,768,512]{2,0,1:T(2,128)(2,1)} copy(bf16[2,768,512]{1,2,0:T(8,128)(2,1)S(1)} %fusion.10) | data formatting | bytes 3145728 | tf_op jit(solution)/shard_map/convert_element_type | solution.py:72
  53.9 4.5 %all-to-all-start.1 = ((bf16[2,768,512]{2,0,1:T(2,128)(2,1)}), bf16[2,768,512]{2,0,1:T(2,128)(2,1)}, u32[]{:S(2)}, u32[]{:S(2)}) async-start(bf16[2,768,512]{2,0,1:T(2,128)(2,1)} %copy.26), calls=%async_computation.1 | async-start | bytes 3145728 | tf_op jit(solution)/shard_map/all_to_all | solution.py:71
  58.4 0.1 broadcast_divide_fusion
  58.5 0.5 subtract_subtract_fusion
  59.0 5.9 %fusion.24 = f32[2,192,16,128]{3,2,1,0:T(8,128)} fusion(f32[128,128]{1,0:T(8,128)S(1)} %copy-done.1, f32[2,192,16,128]{3,2,1,0:T(8,128)} %param.7, f32[2,192,16,128]{3,2,1,0:T(8,128)} %param.8), kind=kOutput, calls=%fused_computation.34 | convolution fusion | flops 1209532416 | bytes 9502720 | tf_op jit(solution)/shard_map/acij,kj->acik/dot_general | solution.py:37
  64.9 13.5 %all-to-all-done.1 = bf16[2,768,512]{2,0,1:T(2,128)(2,1)} async-done(((bf16[2,768,512]{2,0,1:T(2,128)(2,1)}), bf16[2,768,512]{2,0,1:T(2,128)(2,1)}, u32[]{:S(2)}, u32[]{:S(2)}) %all-to-all-start.1) | async-done | bytes 1572896 | tf_op jit(solution)/shard_map/all_to_all | solution.py:71
  78.3 1.7 %copy.27 = bf16[2,768,512]{2,1,0:T(8,128)(2,1)S(1)} copy(bf16[2,768,512]{2,0,1:T(2,128)(2,1)} %all-to-all-done.1) | data formatting | bytes 3145728 | tf_op jit(solution)/shard_map/all_to_all | solution.py:71
  80.0 0.4 convert_bitcast_fusion
  80.4 3.7 %copy.28 = f32[2,192,4,512]{3,2,1,0:T(4,128)} copy(f32[2,192,4,512]{3,1,2,0:T(8,128)S(1)} %convert_bitcast_fusion) | data formatting | bytes 6291456 | tf_op jit(solution)/shard_map/convert_element_type | solution.py:75
  84.1 5.1 %reshape.179 = f32[2,192,16,128]{3,2,1,0:T(8,128)} reshape(f32[2,192,4,512]{3,2,1,0:T(4,128)} %copy.28) | data formatting | bytes 6291456 | tf_op jit(solution)/shard_map/convert_element_type | solution.py:75
  89.2 0.0 copy-start.3
  89.2 0.0 collective-permute-done
  89.2 0.0 collective-permute-done.1
  89.3 7.6 %fusion.7 = f32[2,192,16,128]{3,2,1,0:T(8,128)S(1)} fusion(f32[2,192,16,128]{3,2,1,0:T(8,128)} %reshape.179, f32[2,192,16,128]{3,2,1,0:T(8,128)} %fusion.24, bf16[2,192,16,128]{3,2,1,0:T(8,128)(2,1)} %collective-permute-done.1, bf16[2,192,16,128]{3,2,1,0:T(8,128)(2,1)} %fusion.45, bf16[2,192,16,128]{3,2,1,0:T(8,128)(2,1)} %collective-permute-done, ...), kind=kOutput, calls=%fused_computation.10 | convolution fusion | flops 471859200 | bytes 22028292 | tf_op jit(solution)/shard_map/ij,acjk->acik/dot_general | solution.py:42
  96.8 0.0 copy-done.3
  96.8 0.3 fusion.46
  97.1 0.0 copy-start.4
  97.1 1.7 %copy-done.4 = f32[2,192,16,128]{3,2,1,0:T(8,128)} copy-done((f32[2,192,16,128]{3,2,1,0:T(8,128)}, f32[2,192,16,128]{3,2,1,0:T(8,128)S(1)}, u32[]{:S(2)}) %copy-start.4) | copy-done | bytes 3145752
  (14 shorter events, 0.1 us)
Async XLA Ops:
  0.0 48.2 %copy-start = (bf16[768,768]{1,0:T(8,128)(2,1)S(1)}, bf16[768,768]{1,0:T(8,128)(2,1)}, u32[]{:S(2)}) copy-start(bf16[768,768]{1,0:T(8,128)(2,1)} %param.10) | copy-start | bytes 3538948
  4.5 84.8 %collective-permute-start = (bf16[2,192,16,128]{3,2,1,0:T(8,128)(2,1)}, bf16[2,192,16,128]{3,2,1,0:T(8,128)(2,1)}, u32[]{:S(2)}, u32[]{:S(2)}) collective-permute-start(bf16[2,192,16,128]{3,2,1,0:T(8,128)(2,1)} %fusion.45), channel_id=1, source_target_pairs={{0,1},{1,2},{2,3},{3,4},{4,5},{5,6},{6,7},{8,9},{9,10},{10,11},{11... | collective-permute-start | bytes 4718600 | tf_op jit(solution)/shard_map/ppermute | solution.py:20
  10.6 78.7 %collective-permute-start.1 = (bf16[2,192,16,128]{3,2,1,0:T(8,128)(2,1)}, bf16[2,192,16,128]{3,2,1,0:T(8,128)(2,1)}, u32[]{:S(2)}, u32[]{:S(2)}) collective-permute-start(bf16[2,192,16,128]{3,2,1,0:T(8,128)(2,1)} %fusion.45), channel_id=1, source_target_pairs={{1,0},{2,1},{3,2},{4,3},{5,4},{6,5},{7,6},{9,8},{10,9},{11,10},{12... | collective-permute-start | bytes 4718600 | tf_op jit(solution)/shard_map/ppermute | solution.py:21
  14.6 5.6 %copy-start.2 = (s32[192,2]{0,1:T(2,128)S(1)}, s32[192,2]{0,1:T(2,128)}, u32[]{:S(2)}) copy-start(s32[192,2]{0,1:T(2,128)} %param.12) | copy-start | bytes 4612
  14.6 5.7 %copy-start.1 = (f32[128,128]{1,0:T(8,128)S(1)}, f32[128,128]{1,0:T(8,128)}, u32[]{:S(2)}) copy-start(f32[128,128]{1,0:T(8,128)} %param.11) | copy-start | bytes 196612
  15.9 23.6 %all-to-all-start = ((bf16[4,2,192,512]{3,2,1,0:T(8,128)(2,1)}), bf16[4,2,192,512]{3,2,1,0:T(8,128)(2,1)S(1)}, u32[]{:S(2)}, u32[]{:S(2)}) async-start(bf16[4,2,192,512]{3,2,1,0:T(8,128)(2,1)} %pad_maximum_fusion.1), calls=%async_computation | async-start | bytes 3145728 | tf_op jit(solution)/shard_map/all_to_all | solution.py:9
  39.5 5.8 %slice-start = ((s8[4718592]{0:T(1024)(128)(4,1)}), s8[4194304]{0:T(1024)(128)(4,1)S(1)}, s32[]{:S(2)}) async-start(s8[4718592]{0:T(1024)(128)(4,1)} %bitcast.71), calls=%async_computation.2 | async-start | bytes 8388608
  39.7 5.6 %slice-start.1 = ((s8[4718592]{0:T(1024)(128)(4,1)}), s8[524288]{0:T(1024)(128)(4,1)S(1)}, s32[]{:S(2)}) async-start(s8[4718592]{0:T(1024)(128)(4,1)} %bitcast.71), calls=%async_computation.3 | async-start | bytes 1048576
  53.9 24.5 %all-to-all-start.1 = ((bf16[2,768,512]{2,0,1:T(2,128)(2,1)}), bf16[2,768,512]{2,0,1:T(2,128)(2,1)}, u32[]{:S(2)}, u32[]{:S(2)}) async-start(bf16[2,768,512]{2,0,1:T(2,128)(2,1)} %copy.26), calls=%async_computation.1 | async-start | bytes 3145728 | tf_op jit(solution)/shard_map/all_to_all | solution.py:71
  89.2 7.6 %copy-start.3 = (f32[2,192,16,128]{3,2,1,0:T(8,128)S(1)}, f32[2,192,16,128]{3,2,1,0:T(8,128)}, u32[]{:S(2)}) copy-start(f32[2,192,16,128]{3,2,1,0:T(8,128)} %custom-call) | copy-start | bytes 9437188
  97.1 1.7 %copy-start.4 = (f32[2,192,16,128]{3,2,1,0:T(8,128)}, f32[2,192,16,128]{3,2,1,0:T(8,128)S(1)}, u32[]{:S(2)}) copy-start(f32[2,192,16,128]{3,2,1,0:T(8,128)S(1)} %get-tuple-element.21) | copy-start | bytes 9437188
